TPU v7x, 768 devices: a whole 4x8x12 slice. The times are simulated.
768 devices in a mesh: rep: 16 (over y, x_lo), row: 4 (over x_hi, core), col: 12 (over z).
Axes of the slice: x: 4 (x_hi: 2, x_lo: 2; x = x_hi * 2 + x_lo), y: 8, z: 12, core: 2. Of those that a mesh axis runs over, the one named last changes fastest.
Arguments:
- tokens: bfloat16 [24576, 4096], P('rep', 'row'), may hold values from -6 to 6
- cotangent: bfloat16 [24576, 1536], P(('rep', 'row'), 'col'), may hold values from -4 to 4
- weight: float32 [16, 4096, 1536], P('rep', 'row', 'col'), may hold values from -0.09375 to 0.09375
- first_moment: float32 [16, 4096, 1536], P('rep', 'row', 'col'), may hold values from -6 to 6
- second_moment: float32 [16, 4096, 1536], P('rep', 'row', 'col'), may hold values from 1 to 10
- outer_delta: float32 [16, 7864320], P('rep', ('row', 'col')), may hold values from -6 to 6
- global_params: float32 [2, 7864320], P(None, ('row', 'col')), may hold values from -6 to 6
- outer_moment: float32 [2, 7864320], P(None, ('row', 'col')), may hold values from -6 to 6
- group_slot: int32 [1], replicated, may hold values from 0 to 1
Outputs:
- keys_values: bfloat16 [24576, 1536], P(('rep', 'row'), 'col')
- input_grad: bfloat16 [24576, 4096], P(('rep', 'col'), 'row')
- new_weight: float32 [16, 4096, 1536], P('rep', 'row', 'col')
- new_first: float32 [16, 4096, 1536], P('rep', 'row', 'col')
- new_second: float32 [16, 4096, 1536], P('rep', 'row', 'col')
- new_global: float32 [7864320], P(('row', 'col'))
- new_outer: float32 [7864320], P(('row', 'col'))
Inputs may be any that keep to these rules, and one draw needn't show every extreme that they name: `group_slot`: the held group that the outer delta belongs to.
All inputs are finite; a program needn't handle non-finite values.
Results may differ from a plain program's by a relative error of at most 0.015.
Values may be sent and summed in bfloat16 or wider, within the bound.
A program may use at most 64 MiB of HBM per device.

v0:
```python
import jax
import jax.numpy as jnp
from jax import lax
from jax.sharding import PartitionSpec as P

BETA_ONE = 0.9
BETA_TWO = 0.95
INNER_RATE = 0.0003
WEIGHT_DECAY = 0.1
EPSILON = 1e-08
OUTER_RATE = 0.7
NESTEROV = 0.9


def nesterov_merge(average, held_group, prior_moment):
    new_outer = NESTEROV * prior_moment + average
    new_global = held_group - OUTER_RATE * (average + NESTEROV * new_outer)
    return (new_global, new_outer)


def outer_step(outer_delta, global_params, outer_moment, group_slot):
    chosen = group_slot[0]
    held_group = lax.dynamic_index_in_dim(global_params, chosen, 0, keepdims=False)
    prior_moment = lax.dynamic_index_in_dim(outer_moment, chosen, 0, keepdims=False)
    replicas = lax.axis_size("rep")
    average = lax.psum(outer_delta[0].astype(jnp.bfloat16), "rep").astype(jnp.float32) / replicas
    new_global, new_outer = nesterov_merge(average, held_group, prior_moment)
    return (new_global, new_outer)


def inner_step(tokens, cotangent, weight, first_moment, second_moment):
    weight_bf = weight[0].astype(jnp.bfloat16)
    keys_values = lax.psum_scatter(
        jnp.dot(tokens, weight_bf, preferred_element_type=jnp.float32).astype(jnp.bfloat16),
        "row",
        scatter_dimension=0,
        tiled=True,
    )
    cot_full = lax.all_gather(cotangent, "row", axis=0, tiled=True)
    gradient = jnp.einsum("td,tc->dc", tokens, cot_full, preferred_element_type=jnp.float32)
    input_grad = lax.psum_scatter(
        jnp.einsum("tc,dc->td", cot_full, weight_bf, preferred_element_type=jnp.float32).astype(
            jnp.bfloat16
        ),
        "col",
        scatter_dimension=0,
        tiled=True,
    )
    first_new = BETA_ONE * first_moment[0] + (1.0 - BETA_ONE) * gradient
    second_new = BETA_TWO * second_moment[0] + (1.0 - BETA_TWO) * gradient * gradient
    weight_new = weight[0] - INNER_RATE * (
        first_new / (jnp.sqrt(second_new) + EPSILON) + WEIGHT_DECAY * weight[0]
    )
    return (keys_values, input_grad, weight_new[None], first_new[None], second_new[None])


def on_device(
    tokens,
    cotangent,
    weight,
    first_moment,
    second_moment,
    outer_delta,
    global_params,
    outer_moment,
    group_slot,
):
    keys_values, input_grad, new_weight, new_first, new_second = inner_step(
        tokens, cotangent, weight, first_moment, second_moment
    )
    new_global, new_outer = outer_step(outer_delta, global_params, outer_moment, group_slot)
    return (keys_values, input_grad, new_weight, new_first, new_second, new_global, new_outer)


def solution(mesh):
    in_specs = (
        P("rep", "row"),
        P(("rep", "row"), "col"),
        P("rep", "row", "col"),
        P("rep", "row", "col"),
        P("rep", "row", "col"),
        P("rep", ("row", "col")),
        P(None, ("row", "col")),
        P(None, ("row", "col")),
        P(),
    )
    out_specs = (
        P(("rep", "row"), "col"),
        P(("rep", "col"), "row"),
        P("rep", "row", "col"),
        P("rep", "row", "col"),
        P("rep", "row", "col"),
        P(("row", "col")),
        P(("row", "col")),
    )
    return jax.shard_map(
        on_device, mesh=mesh, in_specs=in_specs, out_specs=out_specs, check_vma=False
    )
```

profile of v0, /device:TPU:6, one launch (start us, length us, event | category | flops | bytes accessed | tf_op | source)
XLA Modules:
  0.0 180.6 jit_solution(10764751913357179688)
XLA Ops:
  8.0 0.0 copy-start
  8.0 0.0 all-reduce.2.cloned.1.call-start
  8.1 8.6 %convert_reduce_fusion = bf16[163840]{0:T(1024)(128)(2,1)} fusion(f32[1,163840]{1,0:T(1,128)} %param.14), kind=kLoop, calls=%fused_computation.7 | loop fusion | flops 163840 | bytes 983040 | tf_op jit(solution)/shard_map/convert_element_type | solution.py:26
  16.7 0.0 all-reduce.2.cloned.1.call-update
  16.7 0.0 reduce-scatter.3.cloned.1.call-start
  16.8 0.0 copy-done
  16.8 2.8 %fusion.10 = bf16[1536,128]{1,0:T(8,128)(2,1)} fusion(bf16[1536,1024]{1,0:T(8,128)(2,1)S(1)} %copy-done, f32[1,1024,128]{2,1,0:T(8,128)} %param.11), kind=kOutput, calls=%fused_computation.19 | convolution fusion | flops 402653184 | bytes 4063232 | tf_op jit(solution)/shard_map/dot_general | solution.py:34
  19.6 0.0 reduce-scatter.3.cloned.1.call-update
  19.6 0.0 reduce-scatter.5.cloned.1.call-start
  19.6 7.9 %all_gather.3 = bf16[1536,128]{1,0:T(8,128)(2,1)S(1)} all-gather(bf16[384,128]{1,0:T(8,128)(2,1)} %param.10), channel_id=1, replica_groups=mesh['rep'=16,'row'=4,'col'=12] {'row'}, dimensions={0}, use_global_device_ids=true | all-gather | bytes 491520 | tf_op jit(solution)/shard_map/all_gather | solution.py:39
  27.5 3.7 %fusion.12 = bf16[1536,1024]{1,0:T(8,128)(2,1)} fusion(bf16[1536,128]{1,0:T(8,128)(2,1)S(1)} %all_gather.3, f32[1,1024,128]{2,1,0:T(8,128)} %param.11), kind=kOutput, calls=%fused_computation.21 | convolution fusion | flops 402653184 | bytes 4063232 | tf_op jit(solution)/shard_map/tc,dc->td/dot_general | solution.py:42
  31.2 0.0 reduce-scatter.5.cloned.1.call-update
  31.9 3.7 %dynamic-slice_multiply_fusion = (f32[1,163840]{1,0:T(1,128)}, f32[1,163840]{1,0:T(1,128)}) fusion(f32[2,163840]{1,0:T(2,128)} %param.16, s32[]{:T(128)S(6)} %select_n.5, f32[2,163840]{1,0:T(2,128)} %param.15), kind=kLoop, calls=%fused_computation.4 | loop fusion | flops 163840 | bytes 2621444 | tf_op jit(solution)/shard_map/mul | solution.py:16
  35.5 3.6 %fusion.6 = (f32[1,1024,128]{2,1,0:T(8,128)}, f32[1,1024,128]{2,1,0:T(8,128)}, f32[1,1024,128]{2,1,0:T(8,128)}) fusion(f32[1,1024,128]{2,1,0:T(8,128)} %param.13, f32[1,1024,128]{2,1,0:T(8,128)} %param.12, f32[1,1024,128]{2,1,0:T(8,128)} %param.11, bf16[1536,1024]{1,0:T(8,128)(2,1)S(1)} %copy-done, bf16[1536,128]{1,0:T(8,128)(2,1)S(1)} %all_gather.3), kind=kOutput, calls=%fused_computation.17 | convolution fusion | flops 404357120 | bytes 6684672 | tf_op jit(solution)/shard_map/td,tc->dc/dot_general | solution.py:40
  39.2 131.4 %all-reduce.2.cloned.1.call-done = bf16[163840]{0:T(1024)(128)(2,1)} async-done(((bf16[163840]{0:T(1024)(128)(2,1)}), bf16[163840]{0:T(1024)(128)(2,1)}) %all-reduce.2.cloned.1.call-update) | async-done | bytes 327696 | tf_op jit(solution)/shard_map/psum | solution.py:26
  170.6 2.6 %multiply_subtract_fusion = (f32[163840]{0:T(1024)}, f32[163840]{0:T(1024)}) fusion(f32[163840]{0:T(1024)} %bitcast.61, bf16[163840]{0:T(1024)(128)(2,1)} %all-reduce.2.cloned.1.call-done, f32[163840]{0:T(1024)} %bitcast.60), kind=kLoop, calls=%fused_computation.3 | loop fusion | flops 1146880 | bytes 2949120 | tf_op jit(solution)/shard_map/sub | solution.py:17
  173.2 0.0 reduce-scatter.3.cloned.1.call-done
  173.2 0.0 reduce-scatter.5.cloned.1.call-done
Async XLA Ops:
  8.0 8.8 %copy-start = (bf16[1536,1024]{1,0:T(8,128)(2,1)S(1)}, bf16[1536,1024]{1,0:T(8,128)(2,1)}, u32[]{:S(2)}) copy-start(bf16[1536,1024]{1,0:T(8,128)(2,1)} %param.9) | copy-start | bytes 9437188
  8.0 162.6 %all-reduce.2.cloned.1.call-start = ((), (), s32[]{:S(2)}) async-start(), calls=%async_computation.4 | async-start | bytes 655360 | tf_op jit(solution)/shard_map/psum | solution.py:26
  16.7 156.5 %reduce-scatter.3.cloned.1.call-start = ((), (), s32[]{:S(2)}) async-start(), calls=%async_computation.2 | async-start | bytes 491520 | tf_op jit(solution)/shard_map/reduce_scatter | solution.py:33
  19.6 153.6 %reduce-scatter.5.cloned.1.call-start = ((), (), s32[]{:S(2)}) async-start(), calls=%async_computation.3 | async-start | bytes 3407872 | tf_op jit(solution)/shard_map/reduce_scatter | solution.py:41
Sparse Core Ops, SparseCore 0:
  16.8 153.7 all-reduce.1
Sparse Core Ops, SparseCore 1:
  21.1 49.3 reduce-scatter.2
  74.0 66.6 reduce-scatter.4
where the time goes:
time: 181 us
  waiting for transfers between devices  131 us (72%)
  between operations  16.2 us (9%)
  other arithmetic  14.9 us (8%)
  matrix products  10.1 us (6%)
  blocking collectives  7.86 us (4%)
    psum x1, waiting for transfers between devices, outer_step(): lax.psum(outer_delta[0].astype(jnp.bfloat16), 'rep').astype(jnp.float32)  131 us
    convert_element_type x1, other arithmetic, outer_step(): outer_delta[0].astype(jnp.bfloat16)  8.65 us
    all_gather x1, blocking collectives, inner_step(): cot_full = lax.all_gather(cotangent, 'row', axis=0, tiled=True)  7.86 us
    dot_general x1, matrix products, inner_step(): jnp.einsum('tc,dc->td', cot_full, weight_bf, preferred_element_type=jnp.f...  3.68 us
    mul x1, other arithmetic, nesterov_merge(): new_outer = NESTEROV * prior_moment + average  3.67 us
    dot_general x1, matrix products, inner_step(): jnp.einsum('td,tc->dc', tokens, cot_full, preferred_element_type=jnp.floa...  3.64 us
  transfers between devices with their start and end apart: 3, of which 1 were waited for; matrix products, arithmetic and copies ran while one was open for 9% of the time, Pallas kernels for 0%

commit v1 on v0

v1 whole, which is shorter than its diff:
```python
import functools

import jax
import jax.numpy as jnp
from jax import lax
from jax.experimental import pallas as pl
from jax.experimental.pallas import tpu as pltpu
from jax.sharding import PartitionSpec as P

BETA_ONE = 0.9
BETA_TWO = 0.95
INNER_RATE = 0.0003
WEIGHT_DECAY = 0.1
EPSILON = 1e-08
OUTER_RATE = 0.7
NESTEROV = 0.9

MESH = pl.DeviceIdType.MESH
F32 = jnp.float32
BF16 = jnp.bfloat16
LANES = 128


def step_kernel(
    sizes,
    x_hbm,
    g_hbm,
    w_hbm,
    m_hbm,
    v_hbm,
    od_hbm,
    gp_hbm,
    om_hbm,
    slot_ref,
    kv_o,
    ig_o,
    w_o,
    m_o,
    v_o,
    ng_o,
    no_o,
    x_v,
    g_v,
    w_v,
    wb_v,
    m_v,
    v_v,
    od_v,
    gp_v,
    om_v,
    kvp,
    kvr,
    kvf,
    zs_buf,
    zr_buf,
    ig_v,
    ob,
    xr,
    hs,
    yr,
    of,
    ld,
    st,
    gs,
    gr,
    ks,
    kr,
    zs,
    zr,
    xs,
    xrs,
    ys,
    yrs,
):
    nrep, nrow, ncol = sizes
    ny = nrep // 2
    rep = lax.axis_index("rep")
    row = lax.axis_index("row")
    col = lax.axis_index("col")
    yy = rep // 2
    xlo = rep % 2

    tok = x_v.shape[0]
    feat = x_v.shape[1]
    rtok = tok // nrow
    blk = tok // ncol
    per_row = ncol // nrow
    fh = feat // 2
    orow = od_v.shape[0]
    half = orow // 2
    piece = half // ny

    row_peer = {1: row + 1 - 2 * (row % 2), 2: (row + 2) % 4, 3: 3 - row}
    right = (col + 1) % ncol
    left = (col + ncol - 1) % ncol
    xmate = rep + 1 - 2 * xlo
    ypeer = {d: ((yy + d) % ny) * 2 + xlo for d in range(1, ny)}

    barrier = pltpu.get_barrier_semaphore()
    count = 0
    for d in (1, 2, 3):
        pl.semaphore_signal(barrier, inc=1, device_id=(rep, row_peer[d], col), device_id_type=MESH)
        count += 1
    for c in (left, right):
        pl.semaphore_signal(barrier, inc=1, device_id=(rep, row, c), device_id_type=MESH)
        count += 1
    for d in range(1, ny):
        pl.semaphore_signal(barrier, inc=1, device_id=(ypeer[d], row, col), device_id_type=MESH)
        count += 1
    pl.semaphore_signal(barrier, inc=1, device_id=(xmate, row, col), device_id_type=MESH)
    count += 1

    own_rows = pl.ds(pl.multiple_of(row * rtok, rtok), rtok)
    loads = {
        "w": pltpu.make_async_copy(w_hbm, w_v, ld.at[0]),
        "g": pltpu.make_async_copy(g_hbm, g_v.at[own_rows], ld.at[1]),
        "x": pltpu.make_async_copy(x_hbm, x_v, ld.at[2]),
        "od": pltpu.make_async_copy(od_hbm, od_v, ld.at[3]),
        "m": pltpu.make_async_copy(m_hbm, m_v, ld.at[4]),
        "v": pltpu.make_async_copy(v_hbm, v_v, ld.at[5]),
        "gp0": pltpu.make_async_copy(gp_hbm.at[:, 0, :], gp_v.at[0], ld.at[6]),
        "gp1": pltpu.make_async_copy(gp_hbm.at[:, 1, :], gp_v.at[1], ld.at[7]),
        "om0": pltpu.make_async_copy(om_hbm.at[:, 0, :], om_v.at[0], ld.at[8]),
        "om1": pltpu.make_async_copy(om_hbm.at[:, 1, :], om_v.at[1], ld.at[9]),
    }
    for name in ("w", "g", "x", "od", "m", "v", "gp0", "gp1", "om0", "om1"):
        loads[name].start()

    loads["w"].wait()
    wb_v[...] = w_v[...].astype(BF16)
    pl.semaphore_wait(barrier, count)

    sends = []

    c = (col + ncol // 2 + ncol - per_row * row) % ncol
    if per_row == 3:
        first = jnp.where(c == 0, 0, jnp.where(c == 1, 1, jnp.where(c <= 7, 2, 0)))
        second = jnp.where(first == 1, 0, 1)
        order = (first, second, 3 - first - second)
    else:
        order = tuple(range(per_row))
    for n, j in enumerate(order):
        at = per_row * row + j
        for d in (2, 3, 1):
            copy = pltpu.make_async_remote_copy(
                src_ref=g_hbm.at[pl.ds(pl.multiple_of(j * blk, blk), blk)],
                dst_ref=g_v.at[pl.ds(pl.multiple_of(at * blk, blk), blk)],
                send_sem=gs.at[n, d - 1],
                recv_sem=gr.at[at],
                device_id=(rep, row_peer[d], col),
                device_id_type=MESH,
            )
            copy.start()
            sends.append(copy)

    loads["x"].wait()
    kv_copies = {}
    for d in (2, 3, 1, 0):
        to = row_peer[d] if d else row
        rows = pl.ds(pl.multiple_of(to * rtok, rtok), rtok)
        part = jnp.dot(x_v[rows, :], wb_v[...], preferred_element_type=F32)
        kvp[d] = part.astype(BF16)
        if d:
            copy = pltpu.make_async_remote_copy(
                src_ref=kvp.at[d],
                dst_ref=kvr.at[d - 1],
                send_sem=ks.at[d - 1],
                recv_sem=kr.at[d - 1],
                device_id=(rep, row_peer[d], col),
                device_id_type=MESH,
            )
            copy.start()
            sends.append(copy)
            kv_copies[d] = copy
    loads["g"].wait()

    def await_block(t):
        rows = pl.ds(pl.multiple_of(t * blk, blk), blk)

        @pl.when(t // per_row != row)
        def _():
            pltpu.make_async_remote_copy(
                src_ref=g_v.at[rows],
                dst_ref=g_v.at[rows],
                send_sem=gs.at[0, 0],
                recv_sem=gr.at[t],
                device_id=(rep, row_peer[1], col),
                device_id_type=MESH,
            ).wait_recv()

    waited = set()

    def need(offset):
        if offset % ncol not in waited:
            waited.add(offset % ncol)
            await_block((col + offset + ncol) % ncol)

    def contribution(t, h):
        rows = pl.ds(pl.multiple_of(t * blk, blk), blk)
        return lax.dot_general(
            g_v[rows, :],
            wb_v[h * fh : (h + 1) * fh, :],
            (((1,), (1,)), ((), ())),
            preferred_element_type=F32,
        )

    long, short = ncol // 2, ncol - 1 - ncol // 2
    chains = ((0, 0, long), (1, 1, long), (0, 1, short), (1, 0, short))

    ostores = []
    xcopies = {}
    ycopies = {}
    chunk = 80 if piece % 80 == 0 else piece

    def outer_first():
        loads["od"].wait()

        @pl.loop(0, half // chunk)
        def _(i):
            src = pl.ds(pl.multiple_of((1 - xlo) * half + i * chunk, chunk), chunk)
            dst = pl.ds(pl.multiple_of(i * chunk, chunk), chunk)
            ob[dst, :] = od_v[src, :].astype(BF16)

        copy = pltpu.make_async_remote_copy(
            src_ref=ob,
            dst_ref=xr,
            send_sem=xs.at[0],
            recv_sem=xrs.at[0],
            device_id=(xmate, row, col),
            device_id_type=MESH,
        )
        copy.start()
        sends.append(copy)
        xcopies[0] = copy

    def outer_scatter():
        xcopies[0].wait_recv()

        @pl.loop(0, half // chunk)
        def _(i):
            src = pl.ds(pl.multiple_of(xlo * half + i * chunk, chunk), chunk)
            dst = pl.ds(pl.multiple_of(i * chunk, chunk), chunk)
            hs[dst, :] = (od_v[src, :] + xr[dst, :].astype(F32)).astype(BF16)

        for d in range(1, ny):
            to = (yy + d) % ny
            copy = pltpu.make_async_remote_copy(
                src_ref=hs.at[pl.ds(pl.multiple_of(to * piece, piece), piece)],
                dst_ref=yr.at[d - 1],
                send_sem=ys.at[0, d - 1],
                recv_sem=yrs.at[0, d - 1],
                device_id=(ypeer[d], row, col),
                device_id_type=MESH,
            )
            copy.start()
            sends.append(copy)
            ycopies[0, d] = copy

    def outer_gather():
        mine = pl.ds(pl.multiple_of(yy * piece, piece), piece)
        total = hs[mine, :].astype(F32)
        for d in range(1, ny):
            ycopies[0, d].wait_recv()
            total = total + yr[d - 1].astype(F32)
        of[xlo, mine, :] = total.astype(BF16)
        for d in range(1, ny):
            copy = pltpu.make_async_remote_copy(
                src_ref=of.at[xlo, mine],
                dst_ref=of.at[xlo, mine],
                send_sem=ys.at[1, d - 1],
                recv_sem=yrs.at[1, d - 1],
                device_id=(ypeer[d], row, col),
                device_id_type=MESH,
            )
            copy.start()
            sends.append(copy)

    def outer_last():
        for d in range(1, ny):
            there = pl.ds(pl.multiple_of(((yy + ny - d) % ny) * piece, piece), piece)
            pltpu.make_async_remote_copy(
                src_ref=of.at[xlo, there],
                dst_ref=of.at[xlo, there],
                send_sem=ys.at[1, d - 1],
                recv_sem=yrs.at[1, d - 1],
                device_id=(ypeer[d], row, col),
                device_id_type=MESH,
            ).wait_recv()
        copy = pltpu.make_async_remote_copy(
            src_ref=of.at[xlo],
            dst_ref=of.at[xlo],
            send_sem=xs.at[1],
            recv_sem=xrs.at[1],
            device_id=(xmate, row, col),
            device_id_type=MESH,
        )
        copy.start()
        sends.append(copy)

    def outer_merge():
        pltpu.make_async_remote_copy(
            src_ref=of.at[1 - xlo],
            dst_ref=of.at[1 - xlo],
            send_sem=xs.at[1],
            recv_sem=xrs.at[1],
            device_id=(xmate, row, col),
            device_id_type=MESH,
        ).wait_recv()
        for name in ("gp0", "gp1", "om0", "om1"):
            loads[name].wait()
        second = slot_ref[0] == 1
        for q in range(2):

            @pl.loop(0, half // chunk)
            def _(i):
                here = pl.ds(pl.multiple_of(i * chunk, chunk), chunk)
                full = pl.ds(pl.multiple_of(q * half + i * chunk, chunk), chunk)
                average = of[q, here, :].astype(F32) * (1.0 / nrep)
                prior = jnp.where(second, om_v[1, full, :], om_v[0, full, :])
                held = jnp.where(second, gp_v[1, full, :], gp_v[0, full, :])
                new_outer = NESTEROV * prior + average
                om_v[0, full, :] = new_outer
                gp_v[0, full, :] = held - OUTER_RATE * (average + NESTEROV * new_outer)

        for n, (src, dst) in enumerate(((gp_v, ng_o), (om_v, no_o))):
            copy = pltpu.make_async_copy(src.at[0], dst, st.at[n])
            copy.start()
            ostores.append(copy)

    def keys_values():
        for d in (1, 2, 3):
            kv_copies[d].wait_recv()
        total = kvp[0].astype(F32)
        for d in (1, 2, 3):
            total = total + kvr[d - 1].astype(F32)
        kvf[...] = total.astype(BF16)
        copy = pltpu.make_async_copy(kvf, kv_o, st.at[2])
        copy.start()
        ostores.append(copy)

    gc = 256 if feat % 1024 == 0 else feat // 4

    def optimizer(i):
        def run():
            if i == 0:
                loads["m"].wait()
                loads["v"].wait()
                for j in range(ncol):
                    need(j)
            cols = slice(i * gc, (i + 1) * gc)
            grad = lax.dot_general(
                x_v[:, cols], g_v[...], (((0,), (0,)), ((), ())), preferred_element_type=F32
            )
            first = BETA_ONE * m_v[cols, :] + (1.0 - BETA_ONE) * grad
            second = BETA_TWO * v_v[cols, :] + (1.0 - BETA_TWO) * grad * grad
            m_v[cols, :] = first
            v_v[cols, :] = second
            held = w_v[cols, :]
            w_v[cols, :] = held - INNER_RATE * (first / (jnp.sqrt(second) + EPSILON) + WEIGHT_DECAY * held)
            for n, (src, dst) in enumerate(((w_v, w_o), (m_v, m_o), (v_v, v_o))):
                copy = pltpu.make_async_copy(src.at[cols], dst.at[cols], st.at[3 + 3 * i + n])
                copy.start()
                ostores.append(copy)

        return run

    fill = {
        0: outer_first,
        4: outer_scatter,
        6: keys_values,
        8: outer_gather,
        9: optimizer(0),
        10: optimizer(1),
        11: optimizer(2),
        12: outer_last,
        13: optimizer(3),
        17: outer_merge,
    }
    if ncol != 12:
        plan = list(fill.values())
        fill = {}

    def chain_copy(n, way, k, src):
        return pltpu.make_async_remote_copy(
            src_ref=src,
            dst_ref=zr_buf.at[n, k],
            send_sem=zs.at[n, k],
            recv_sem=zr.at[n, k],
            device_id=(rep, row, right if way == 0 else left),
            device_id_type=MESH,
        )

    slot = 0
    for k in range(long):
        for n, (way, h, length) in enumerate(chains):
            if k >= length:
                continue
            sign = 1 if way == 0 else -1
            need(sign * (length - k))
            part = contribution((col + sign * (length - k) + ncol) % ncol, h)
            if k == 0:
                zs_buf[n] = part.astype(BF16)
                copy = chain_copy(n, way, k, zs_buf.at[n])
            else:
                chain_copy(n, way, k - 1, zr_buf.at[n, k - 1]).wait_recv()
                zr_buf[n, k - 1] = (zr_buf[n, k - 1].astype(F32) + part).astype(BF16)
                copy = chain_copy(n, way, k, zr_buf.at[n, k - 1])
            copy.start()
            sends.append(copy)
            if slot in fill:
                fill[slot]()
            slot += 1
    if ncol != 12:
        for run in plan:
            run()

    need(0)
    for h, pair in ((0, (0, 3)), (1, (1, 2))):
        part = contribution(col, h)
        for n in pair:
            way, _, length = chains[n]
            chain_copy(n, way, length - 1, zr_buf.at[n, length - 1]).wait_recv()
            part = part + zr_buf[n, length - 1].astype(F32)
        ig_v[:, h * fh : (h + 1) * fh] = part.astype(BF16)
    copy = pltpu.make_async_copy(ig_v, ig_o, st.at[15])
    copy.start()
    ostores.append(copy)
    for copy in sends:
        copy.wait_send()
    for copy in ostores:
        copy.wait()


def on_device(sizes, tokens, cotangent, weight, first_moment, second_moment, outer_delta, global_params, outer_moment, group_slot):
    nrep, nrow, ncol = sizes
    tok, feat = tokens.shape
    rtok = cotangent.shape[0]
    blk = tok // ncol
    hd = cotangent.shape[1]
    orow = outer_delta.shape[1] // LANES
    half = orow // 2
    ny = nrep // 2
    piece = half // ny
    long = ncol // 2
    held = global_params.reshape(2, orow, LANES).transpose(1, 0, 2)
    moment = outer_moment.reshape(2, orow, LANES).transpose(1, 0, 2)
    any_ref = pl.BlockSpec(memory_space=pl.ANY)
    vmem = pltpu.VMEM
    dma = pltpu.SemaphoreType.DMA
    shape = jax.ShapeDtypeStruct
    outs = pl.pallas_call(
        functools.partial(step_kernel, sizes),
        out_shape=(
            shape((rtok, hd), BF16),
            shape((blk, feat), BF16),
            shape((feat, hd), F32),
            shape((feat, hd), F32),
            shape((feat, hd), F32),
            shape((orow, LANES), F32),
            shape((orow, LANES), F32),
        ),
        in_specs=[any_ref] * 8 + [pl.BlockSpec(memory_space=pltpu.SMEM)],
        out_specs=(any_ref,) * 7,
        scratch_shapes=[
            vmem((tok, feat), BF16),
            vmem((tok, hd), BF16),
            vmem((feat, hd), F32),
            vmem((feat, hd), BF16),
            vmem((feat, hd), F32),
            vmem((feat, hd), F32),
            vmem((orow, LANES), F32),
            vmem((2, orow, LANES), F32),
            vmem((2, orow, LANES), F32),
            vmem((4, rtok, hd), BF16),
            vmem((3, rtok, hd), BF16),
            vmem((rtok, hd), BF16),
            vmem((4, blk, feat // 2), BF16),
            vmem((4, long, blk, feat // 2), BF16),
            vmem((blk, feat), BF16),
            vmem((half, LANES), BF16),
            vmem((half, LANES), BF16),
            vmem((half, LANES), BF16),
            vmem((max(ny - 1, 1), piece, LANES), BF16),
            vmem((2, half, LANES), BF16),
            dma((10,)),
            dma((16,)),
            dma((ncol // nrow, 3)),
            dma((ncol,)),
            dma((3,)),
            dma((3,)),
            dma((4, long)),
            dma((4, long)),
            dma((2,)),
            dma((2,)),
            dma((2, max(ny - 1, 1))),
            dma((2, max(ny - 1, 1))),
        ],
        compiler_params=pltpu.CompilerParams(collective_id=0, has_side_effects=True),
        name="diloco_step",
    )(
        tokens,
        cotangent,
        weight[0],
        first_moment[0],
        second_moment[0],
        outer_delta.reshape(orow, LANES),
        held,
        moment,
        group_slot,
    )
    keys_values, input_grad, new_weight, new_first, new_second, new_global, new_outer = outs
    return (
        keys_values,
        input_grad,
        new_weight[None],
        new_first[None],
        new_second[None],
        new_global.reshape(-1),
        new_outer.reshape(-1),
    )


def solution(mesh):
    sizes = (mesh.shape["rep"], mesh.shape["row"], mesh.shape["col"])
    in_specs = (
        P("rep", "row"),
        P(("rep", "row"), "col"),
        P("rep", "row", "col"),
        P("rep", "row", "col"),
        P("rep", "row", "col"),
        P("rep", ("row", "col")),
        P(None, ("row", "col")),
        P(None, ("row", "col")),
        P(),
    )
    out_specs = (
        P(("rep", "row"), "col"),
        P(("rep", "col"), "row"),
        P("rep", "row", "col"),
        P("rep", "row", "col"),
        P("rep", "row", "col"),
        P(("row", "col")),
        P(("row", "col")),
    )
    return jax.shard_map(
        functools.partial(on_device, sizes), mesh=mesh, in_specs=in_specs, out_specs=out_specs, check_vma=False
    )
```

time: 181 us -> 70.1 us (0.39)
  waiting for transfers between devices: 131 us -> 0 us
  Pallas kernels: 0 us -> 59 us
  other arithmetic: 14.9 us -> 0 us
  between operations: 16.2 us -> 1.3 us
  matrix products: 10.1 us -> 0 us
  local copies, waits for them, and re-layouts: 0.01 us -> 8.55 us
  blocking collectives: 7.86 us -> 0 us
    psum x1 -> x0, waiting for transfers between devices: 131 us -> none  [outer_step(): lax.psum(outer_delta[0].astype(jnp.bfloat16), 'rep').astype(jnp.float32)]
    pallas_call x0 -> x1, Pallas kernels: none -> 59 us  [on_device(): pl.pallas_call(functools.partial(step_kernel, sizes), out_shape=(shape((r...]
    dot_general x3 -> x0, matrix products: 10.1 us -> none  [the longest x1 3.68 us: inner_step(): jnp.einsum('tc,dc->td', cot_full, weight_bf, preferred_element_type=jnp.f...]
    convert_element_type x1 -> x0, other arithmetic: 8.65 us -> none  [outer_step(): outer_delta[0].astype(jnp.bfloat16)]
    unnamed x2 -> x15, local copies, waits for them, and re-layouts: 0.01 us -> 8.55 us
    all_gather x1 -> x0, blocking collectives: 7.86 us -> none  [inner_step(): cot_full = lax.all_gather(cotangent, 'row', axis=0, tiled=True)]
    mul x1 -> x0, other arithmetic: 3.67 us -> none  [nesterov_merge(): new_outer = NESTEROV * prior_moment + average]
    sub x1 -> x0, other arithmetic: 2.59 us -> none  [nesterov_merge(): new_global = held_group - OUTER_RATE * (average + NESTEROV * new_outer)]
  transfers between devices with their start and end apart: 3 -> 0, of which waited for: 1 -> 0; matrix products, arithmetic and copies ran while one was open for 9% -> 0% of each run, Pallas kernels for 0% -> 0%
where the time goes in v1:
time: 70.1 us; the launch traced here: 68.8 us
  Pallas kernels  59 us (84%)
  local copies, waits for them, and re-layouts  8.55 us (12%)
  between operations  1.3 us (2%)
    pallas_call x1, Pallas kernels, on_device(): pl.pallas_call(functools.partial(step_kernel, sizes), out_shape=(shape((r...  59 us
    unnamed x15, local copies, waits for them, and re-layouts  8.55 us

profile of v1, /device:TPU:6, one launch (start us, length us, event | category | flops | bytes accessed | tf_op | source)
XLA Modules:
  0.0 68.8 jit_solution(12925055766849598682)
XLA Ops:
  1.3 59.0 %diloco_step.1 = (bf16[384,128]{1,0:T(8,128)(2,1)}, bf16[128,1024]{1,0:T(8,128)(2,1)}, f32[1024,128]{1,0:T(8,128)}, f32[1024,128]{1,0:T(8,128)}, f32[1024,128]{1...) custom-call(bf16[1536,1024]{1,0:T(8,128)(2,1)} %x_hbm.1, bf16[384,128]{1,0:T(8,128)(2,1)} %g_hbm.1, ...), custom_call_target="tpu_custom_call" | custom-call | tf_op jit(solution)/shard_map/diloco_step/pallas_call | solution.py:451
  60.2 0.0 copy-start.3
  60.3 1.6 %copy.24 = bf16[384,128]{1,0:T(8,128)(2,1)} copy(bf16[384,128]{1,0:T(8,128)(2,1)} %get-tuple-element.28) | data formatting | bytes 196608
  61.9 0.0 copy-start.2
  61.9 1.7 %copy.25 = bf16[128,1024]{1,0:T(8,128)(2,1)} copy(bf16[128,1024]{1,0:T(8,128)(2,1)} %get-tuple-element.29) | data formatting | bytes 524288
  63.6 1.9 %copy.26 = f32[1,1024,128]{2,1,0:T(8,128)} copy(f32[1,1024,128]{2,1,0:T(8,128)} %bitcast.25) | data formatting | bytes 1048576
  65.5 0.0 copy-done.3
  65.5 0.0 copy-start.1
  65.5 0.8 %copy.27 = f32[1,1024,128]{2,1,0:T(8,128)} copy(f32[1,1024,128]{2,1,0:T(8,128)S(1)} %bitcast.24) | data formatting | bytes 1048576
  66.2 0.0 copy-done.2
  66.3 0.0 copy-start
  66.3 0.8 %copy.28 = f32[1,1024,128]{2,1,0:T(8,128)} copy(f32[1,1024,128]{2,1,0:T(8,128)S(1)} %bitcast.23) | data formatting | bytes 1048576
  67.0 0.0 copy-done.1
  67.0 0.9 %copy.29 = f32[163840]{0:T(1024)} copy(f32[163840]{0:T(1024)S(1)} %bitcast.19) | data formatting | bytes 1310720
  67.9 0.0 copy-done
  67.9 0.9 %copy.30 = f32[163840]{0:T(1024)} copy(f32[163840]{0:T(1024)S(1)} %bitcast.18) | data formatting | bytes 1310720
Async XLA Ops:
  60.2 5.2 %copy-start.3 = (f32[1024,128]{1,0:T(8,128)S(1)}, f32[1024,128]{1,0:T(8,128)}, u32[]{:S(2)}) copy-start(f32[1024,128]{1,0:T(8,128)} %get-tuple-element.17) | copy-start | bytes 1572868
  61.9 4.4 %copy-start.2 = (f32[1024,128]{1,0:T(8,128)S(1)}, f32[1024,128]{1,0:T(8,128)}, u32[]{:S(2)}) copy-start(f32[1024,128]{1,0:T(8,128)} %get-tuple-element.18) | copy-start | bytes 1572868
  65.5 1.6 %copy-start.1 = (f32[1280,128]{1,0:T(8,128)S(1)}, f32[1280,128]{1,0:T(8,128)}, u32[]{:S(2)}) copy-start(f32[1280,128]{1,0:T(8,128)} %get-tuple-element.19) | copy-start | bytes 1966084
  66.3 1.7 %copy-start = (f32[1280,128]{1,0:T(8,128)S(1)}, f32[1280,128]{1,0:T(8,128)}, u32[]{:S(2)}) copy-start(f32[1280,128]{1,0:T(8,128)} %get-tuple-element.20) | copy-start | bytes 1966084

commit v2 on v1

v2 whole, which is shorter than its diff:
```python
import functools

import jax
import jax.numpy as jnp
from jax import lax
from jax.experimental import pallas as pl
from jax.experimental.pallas import tpu as pltpu
from jax.sharding import PartitionSpec as P

BETA_ONE = 0.9
BETA_TWO = 0.95
INNER_RATE = 0.0003
WEIGHT_DECAY = 0.1
EPSILON = 1e-08
OUTER_RATE = 0.7
NESTEROV = 0.9

MESH = pl.DeviceIdType.MESH
F32 = jnp.float32
BF16 = jnp.bfloat16
LANES = 128
PIECES = 2


def step_kernel(
    sizes,
    x_hbm,
    g_hbm,
    w_hbm,
    m_hbm,
    v_hbm,
    od_hbm,
    gp_hbm,
    om_hbm,
    slot_hbm,
    kv_o,
    ig_o,
    w_o,
    m_o,
    v_o,
    ng_o,
    no_o,
    x_v,
    g_v,
    w_v,
    wb_v,
    m_v,
    v_v,
    od_v,
    gp_v,
    om_v,
    kvp,
    kvr,
    kvx,
    zs_buf,
    zr_buf,
    ob,
    xr,
    hs,
    yr,
    of,
    slot_ref,
    ld,
    gs,
    gr,
    ks,
    kr,
    zs,
    zr,
    xs,
    xrs,
    ys,
    yrs,
):
    nrep, nrow, ncol = sizes
    ny = nrep // 2
    rep = lax.axis_index("rep")
    row = lax.axis_index("row")
    col = lax.axis_index("col")
    yy = rep // 2
    xlo = rep % 2

    tok = x_v.shape[0]
    feat = x_v.shape[1]
    rtok = tok // nrow
    blk = tok // ncol
    per_row = ncol // nrow
    fh = feat // PIECES
    orow = od_v.shape[0]
    piece = orow // ny

    row_peer = {1: row + 1 - 2 * (row % 2), 2: (row + 2) % 4, 3: 3 - row}
    right = (col + 1) % ncol
    left = (col + ncol - 1) % ncol
    xmate = rep + 1 - 2 * xlo
    ypeer = {d: ((yy + d) % ny) * 2 + xlo for d in range(1, ny)}

    barrier = pltpu.get_barrier_semaphore()
    count = 0
    for d in (1, 2, 3):
        pl.semaphore_signal(barrier, inc=1, device_id=(rep, row_peer[d], col), device_id_type=MESH)
        count += 1
    for c in (left, right):
        pl.semaphore_signal(barrier, inc=1, device_id=(rep, row, c), device_id_type=MESH)
        count += 1
    for d in range(1, ny):
        pl.semaphore_signal(barrier, inc=1, device_id=(ypeer[d], row, col), device_id_type=MESH)
        count += 1
    pl.semaphore_signal(barrier, inc=1, device_id=(xmate, row, col), device_id_type=MESH)
    count += 1

    own_rows = pl.ds(pl.multiple_of(row * rtok, rtok), rtok)
    loads = {
        "w": pltpu.make_async_copy(w_hbm, w_v, ld.at[0]),
        "g": pltpu.make_async_copy(g_hbm, g_v.at[own_rows], ld.at[1]),
        "x": pltpu.make_async_copy(x_hbm, x_v, ld.at[2]),
        "od": pltpu.make_async_copy(od_hbm, od_v, ld.at[3]),
        "m": pltpu.make_async_copy(m_hbm, m_v, ld.at[4]),
        "v": pltpu.make_async_copy(v_hbm, v_v, ld.at[5]),
        "gp0": pltpu.make_async_copy(gp_hbm.at[:, 0, :], gp_v.at[0], ld.at[6]),
        "gp1": pltpu.make_async_copy(gp_hbm.at[:, 1, :], gp_v.at[1], ld.at[7]),
        "om0": pltpu.make_async_copy(om_hbm.at[:, 0, :], om_v.at[0], ld.at[8]),
        "om1": pltpu.make_async_copy(om_hbm.at[:, 1, :], om_v.at[1], ld.at[9]),
        "slot": pltpu.make_async_copy(slot_hbm, slot_ref, ld.at[10]),
    }
    for name in ("w", "od", "x", "g", "m", "v", "gp0", "gp1", "om0", "om1", "slot"):
        loads[name].start()

    loads["w"].wait()
    wb_v[...] = w_v[...].astype(BF16)
    pl.semaphore_wait(barrier, count)

    sends = []

    def keep(copy):
        sends.append(copy)
        return copy

    def kv_copy(n, src, d):
        return pltpu.make_async_remote_copy(
            src_ref=src,
            dst_ref=kvr.at[n],
            send_sem=ks.at[n],
            recv_sem=kr.at[n],
            device_id=(rep, row_peer[d], col),
            device_id_type=MESH,
        )

    c = (col + ncol // 2 + ncol - per_row * row) % ncol
    if per_row == 3:
        first = jnp.where(c == 0, 0, jnp.where(c == 1, 1, jnp.where(c <= 7, 2, 0)))
        second = jnp.where(first == 1, 0, 1)
        order = (first, second, 3 - first - second)
    else:
        order = tuple(range(per_row))
    for n, j in enumerate(order):
        at = per_row * row + j
        for d in (2, 3, 1):
            copy = pltpu.make_async_remote_copy(
                src_ref=g_hbm.at[pl.ds(pl.multiple_of(j * blk, blk), blk)],
                dst_ref=g_v.at[pl.ds(pl.multiple_of(at * blk, blk), blk)],
                send_sem=gs.at[n, d - 1],
                recv_sem=gr.at[at],
                device_id=(rep, row_peer[d], col),
                device_id_type=MESH,
            )
            copy.start()
            sends.append(copy)


    def await_block(t):
        rows = pl.ds(pl.multiple_of(t * blk, blk), blk)

        @pl.when(t // per_row != row)
        def _():
            pltpu.make_async_remote_copy(
                src_ref=g_v.at[rows],
                dst_ref=g_v.at[rows],
                send_sem=gs.at[0, 0],
                recv_sem=gr.at[t],
                device_id=(rep, row_peer[1], col),
                device_id_type=MESH,
            ).wait_recv()

    waited = set()

    def need(offset):
        if offset % ncol not in waited:
            waited.add(offset % ncol)
            await_block((col + offset + ncol) % ncol)

    def contribution(t, h):
        rows = pl.ds(pl.multiple_of(t * blk, blk), blk)
        return lax.dot_general(
            g_v[rows, :],
            wb_v[h * fh : (h + 1) * fh, :],
            (((1,), (1,)), ((), ())),
            preferred_element_type=F32,
        )

    long, short = ncol // 2, ncol - 1 - ncol // 2
    chains = tuple(
        ((i + n) % 2, i, long if n == 0 else short) for n in range(2) for i in range(PIECES)
    )

    chunk = 80 if piece % 80 == 0 else piece
    mine = pl.ds(pl.multiple_of(yy * piece, piece), piece)

    def y_copy(stage, d, src, dst):
        return pltpu.make_async_remote_copy(
            src_ref=src,
            dst_ref=dst,
            send_sem=ys.at[stage, d - 1],
            recv_sem=yrs.at[stage, d - 1],
            device_id=(ypeer[d], row, col),
            device_id_type=MESH,
        )

    def x_copy():
        return pltpu.make_async_remote_copy(
            src_ref=hs,
            dst_ref=xr,
            send_sem=xs.at[0],
            recv_sem=xrs.at[0],
            device_id=(xmate, row, col),
            device_id_type=MESH,
        )

    def outer_scatter():
        loads["od"].wait()

        @pl.loop(0, orow // chunk)
        def _(i):
            here = pl.ds(pl.multiple_of(i * chunk, chunk), chunk)
            ob[here, :] = od_v[here, :].astype(BF16)

        for d in range(1, ny):
            to = (yy + d) % ny
            rows = pl.ds(pl.multiple_of(to * piece, piece), piece)
            keep(y_copy(0, d, ob.at[rows], yr.at[d - 1])).start()

    def outer_pair():
        total = od_v[mine, :]
        for d in range(1, ny):
            y_copy(0, d, yr.at[d - 1], yr.at[d - 1]).wait_recv()
            total = total + yr[d - 1].astype(F32)
        hs[...] = total.astype(BF16)
        keep(x_copy()).start()

    def outer_gather():
        x_copy().wait_recv()
        of[mine, :] = (hs[...].astype(F32) + xr[...].astype(F32)).astype(BF16)
        for d in range(1, ny):
            keep(y_copy(1, d, of.at[mine], of.at[mine])).start()

    def outer_merge():
        for d in range(1, ny):
            there = pl.ds(pl.multiple_of(((yy + ny - d) % ny) * piece, piece), piece)
            y_copy(1, d, of.at[there], of.at[there]).wait_recv()
        for name in ("gp0", "gp1", "om0", "om1", "slot"):
            loads[name].wait()
        second = slot_ref[0] == 1

        @pl.loop(0, orow // chunk)
        def _(i):
            here = pl.ds(pl.multiple_of(i * chunk, chunk), chunk)
            average = of[here, :].astype(F32) * (1.0 / nrep)
            prior = jnp.where(second, om_v[1, here, :], om_v[0, here, :])
            held = jnp.where(second, gp_v[1, here, :], gp_v[0, here, :])
            new_outer = NESTEROV * prior + average
            no_o[here, :] = new_outer
            ng_o[here, :] = held - OUTER_RATE * (average + NESTEROV * new_outer)

    def kv_parts(which):
        for d in which:
            to = row_peer[d] if d else row
            rows = pl.ds(pl.multiple_of(to * rtok, rtok), rtok)
            part = jnp.dot(x_v[rows, :], wb_v[...], preferred_element_type=F32)
            kvp[d] = part.astype(BF16)
            if d % 2:
                keep(kv_copy(d // 2, kvp.at[d], 1)).start()

    def kv_cross():
        kv_copy(1, kvr.at[1], 1).wait_recv()
        kvx[...] = (kvp[2].astype(F32) + kvr[1].astype(F32)).astype(BF16)
        keep(kv_copy(2, kvx, 2)).start()

    def keys_values():
        kv_copy(0, kvr.at[0], 1).wait_recv()
        kv_copy(2, kvr.at[2], 2).wait_recv()
        total = kvp[0].astype(F32) + kvr[0].astype(F32) + kvr[2].astype(F32)
        kv_o[...] = total.astype(BF16)

    gc = 256 if feat % 1024 == 0 else feat // 4

    def optimizer(i):
        def run():
            if i == 0:
                loads["m"].wait()
                loads["v"].wait()
                for j in range(ncol):
                    need(j)
            cols = slice(i * gc, (i + 1) * gc)
            grad = lax.dot_general(
                x_v[:, cols], g_v[...], (((0,), (0,)), ((), ())), preferred_element_type=F32
            )
            first = BETA_ONE * m_v[cols, :] + (1.0 - BETA_ONE) * grad
            second = BETA_TWO * v_v[cols, :] + (1.0 - BETA_TWO) * grad * grad
            m_o[cols, :] = first
            v_o[cols, :] = second
            held = w_v[cols, :]
            w_o[cols, :] = held - INNER_RATE * (first / (jnp.sqrt(second) + EPSILON) + WEIGHT_DECAY * held)

        return run

    outer_scatter()
    loads["x"].wait()
    kv_parts((3, 1))
    loads["g"].wait()

    fill = {
        (0, 3): functools.partial(kv_parts, (2, 0)),
        (1, 1): kv_cross,
        (1, 3): outer_pair,
        (2, 1): keys_values,
        (2, 2): optimizer(0),
        (2, 3): outer_gather,
        (3, 0): optimizer(1),
        (3, 1): optimizer(2),
        (3, 2): optimizer(3),
        (4, 2): outer_merge,
    }

    def chain_copy(n, way, k, src):
        return pltpu.make_async_remote_copy(
            src_ref=src,
            dst_ref=zr_buf.at[n, k],
            send_sem=zs.at[n, k],
            recv_sem=zr.at[n, k],
            device_id=(rep, row, right if way == 0 else left),
            device_id_type=MESH,
        )

    for k in range(long):
        for n, (way, h, length) in enumerate(chains):
            if k >= length:
                continue
            sign = 1 if way == 0 else -1
            need(sign * (length - k))
            part = contribution((col + sign * (length - k) + ncol) % ncol, h)
            if k == 0:
                zs_buf[n] = part.astype(BF16)
                copy = chain_copy(n, way, k, zs_buf.at[n])
            else:
                chain_copy(n, way, k - 1, zr_buf.at[n, k - 1]).wait_recv()
                zr_buf[n, k - 1] = (zr_buf[n, k - 1].astype(F32) + part).astype(BF16)
                copy = chain_copy(n, way, k, zr_buf.at[n, k - 1])
            copy.start()
            sends.append(copy)
            at = (k, 2 * n // PIECES)
            if 2 * n % PIECES == 0 and at in fill:
                fill.pop(at)()
    for run in fill.values():
        run()

    need(0)
    for h in range(PIECES):
        part = contribution(col, h)
        for n in (h + PIECES, h):
            way, _, length = chains[n]
            chain_copy(n, way, length - 1, zr_buf.at[n, length - 1]).wait_recv()
            part = part + zr_buf[n, length - 1].astype(F32)
        ig_o[:, h * fh : (h + 1) * fh] = part.astype(BF16)
    for copy in sends:
        copy.wait_send()


def write_kernel(*refs):
    copies = [pltpu.make_async_copy(refs[n], refs[7 + n], refs[14].at[n]) for n in range(7)]
    for copy in copies:
        copy.start()
    for copy in copies:
        copy.wait()


def on_device(sizes, tokens, cotangent, weight, first_moment, second_moment, outer_delta, global_params, outer_moment, group_slot):
    nrep, nrow, ncol = sizes
    tok, feat = tokens.shape
    rtok = cotangent.shape[0]
    blk = tok // ncol
    hd = cotangent.shape[1]
    orow = outer_delta.shape[1] // LANES
    ny = nrep // 2
    piece = orow // ny
    long = ncol // 2
    held = global_params.reshape(2, orow, LANES).transpose(1, 0, 2)
    moment = outer_moment.reshape(2, orow, LANES).transpose(1, 0, 2)
    any_ref = pl.BlockSpec(memory_space=pl.ANY)
    vmem = pltpu.VMEM
    dma = pltpu.SemaphoreType.DMA
    shape = jax.ShapeDtypeStruct
    results = (
        shape((rtok, hd), BF16),
        shape((blk, feat), BF16),
        shape((feat, hd), F32),
        shape((feat, hd), F32),
        shape((feat, hd), F32),
        shape((orow, LANES), F32),
        shape((orow, LANES), F32),
    )
    outs = pl.pallas_call(
        functools.partial(step_kernel, sizes),
        out_shape=[vmem(o.shape, o.dtype) for o in results],
        in_specs=[any_ref] * 8 + [pl.BlockSpec(memory_space=pltpu.HBM)],
        out_specs=[pl.BlockSpec(memory_space=vmem)] * 7,
        scratch_shapes=[
            vmem((tok, feat), BF16),
            vmem((tok, hd), BF16),
            vmem((feat, hd), F32),
            vmem((feat, hd), BF16),
            vmem((feat, hd), F32),
            vmem((feat, hd), F32),
            vmem((orow, LANES), F32),
            vmem((2, orow, LANES), F32),
            vmem((2, orow, LANES), F32),
            vmem((4, rtok, hd), BF16),
            vmem((3, rtok, hd), BF16),
            vmem((rtok, hd), BF16),
            vmem((2 * PIECES, blk, feat // PIECES), BF16),
            vmem((2 * PIECES, long, blk, feat // PIECES), BF16),
            vmem((orow, LANES), BF16),
            vmem((piece, LANES), BF16),
            vmem((piece, LANES), BF16),
            vmem((max(ny - 1, 1), piece, LANES), BF16),
            vmem((orow, LANES), BF16),
            pltpu.SMEM((1,), jnp.int32),
            dma((11,)),
            dma((ncol // nrow, 3)),
            dma((ncol,)),
            dma((3,)),
            dma((3,)),
            dma((2 * PIECES, long)),
            dma((2 * PIECES, long)),
            dma((1,)),
            dma((1,)),
            dma((2, max(ny - 1, 1))),
            dma((2, max(ny - 1, 1))),
        ],
        compiler_params=pltpu.CompilerParams(collective_id=0, has_side_effects=True),
        name="diloco_step",
    )(
        tokens,
        cotangent,
        weight[0],
        first_moment[0],
        second_moment[0],
        outer_delta.reshape(orow, LANES),
        held,
        moment,
        group_slot,
    )
    outs = pl.pallas_call(
        write_kernel,
        out_shape=results,
        in_specs=[pl.BlockSpec(memory_space=vmem)] * 7,
        out_specs=[any_ref] * 7,
        scratch_shapes=[dma((7,))],
        name="write_out",
    )(*(pltpu.with_memory_space_constraint(o, vmem) for o in outs))
    keys_values, input_grad, new_weight, new_first, new_second, new_global, new_outer = outs
    return (
        keys_values,
        input_grad,
        new_weight[None],
        new_first[None],
        new_second[None],
        new_global.reshape(-1),
        new_outer.reshape(-1),
    )


def solution(mesh):
    sizes = (mesh.shape["rep"], mesh.shape["row"], mesh.shape["col"])
    in_specs = (
        P("rep", "row"),
        P(("rep", "row"), "col"),
        P("rep", "row", "col"),
        P("rep", "row", "col"),
        P("rep", "row", "col"),
        P("rep", ("row", "col")),
        P(None, ("row", "col")),
        P(None, ("row", "col")),
        P(),
    )
    out_specs = (
        P(("rep", "row"), "col"),
        P(("rep", "col"), "row"),
        P("rep", "row", "col"),
        P("rep", "row", "col"),
        P("rep", "row", "col"),
        P(("row", "col")),
        P(("row", "col")),
    )
    return jax.shard_map(
        functools.partial(on_device, sizes), mesh=mesh, in_specs=in_specs, out_specs=out_specs, check_vma=False
    )
```

time: 70.1 us -> 58.9 us (0.84)
  local copies, waits for them, and re-layouts: 8.55 us -> 0 us
  Pallas kernels: 59 us -> 56.8 us
    unnamed x15 -> x0, local copies, waits for them, and re-layouts: 8.55 us -> none
    pallas_call x1 -> x2, Pallas kernels: 59 us -> 56.8 us  [the longest x1 55 us: on_device(): pl.pallas_call(functools.partial(step_kernel, sizes), out_shape=[vmem(o.s...]
where the time goes in v2:
time: 58.9 us; the launch traced here: 58.1 us
  Pallas kernels  56.8 us (96%)
  between operations  1.29 us (2%)
    pallas_call x1, Pallas kernels, on_device(): pl.pallas_call(functools.partial(step_kernel, sizes), out_shape=[vmem(o.s...  55 us
    pallas_call x1, Pallas kernels, on_device(): pl.pallas_call(write_kernel, out_shape=results, in_specs=[pl.BlockSpec(me...  1.75 us

profile of v2, /device:TPU:6, one launch (start us, length us, event | category | flops | bytes accessed | tf_op | source)
XLA Modules:
  0.0 58.1 jit_solution(3838969773153551548)
XLA Ops:
  1.3 55.0 %diloco_step.1 = (bf16[384,128]{1,0:T(8,128)(2,1)S(1)}, bf16[128,1024]{1,0:T(8,128)(2,1)S(1)}, f32[1024,128]{1,0:T(8,128)S(1)}, f32[1024,128]{1,0:T(8,128)S(1)},...) custom-call(bf16[1536,1024]{1,0:T(8,128)(2,1)} %x_hbm.1, bf16[384,128]{1,0:T(8,128)(2,1)} %g_hbm.1, ...), custom_call_target="tpu_custom_call" | custom-call | tf_op jit(solution)/shard_map/diloco_step/pallas_call | solution.py:411
  56.3 1.8 %write_out.1 = (bf16[384,128]{1,0:T(8,128)(2,1)}, bf16[128,1024]{1,0:T(8,128)(2,1)}, f32[1024,128]{1,0:T(8,128)}, f32[1024,128]{1,0:T(8,128)}, f32[1024,128]{1,0...) custom-call(bf16[384,128]{1,0:T(8,128)(2,1)S(1)} %get-tuple-element.21.refs_0_, ...), custom_call_target="tpu_custom_call" | custom-call | tf_op jit(solution)/shard_map/write_out/pallas_call | solution.py:462

commit v3 on v2

--- a/solution.py
+++ b/solution.py
@@ -54,6 +54,8 @@
     kvx,
     zs_buf,
     zr_buf,
+    wn_v,
+    gx_v,
     ob,
     xr,
     hs,
@@ -67,6 +69,8 @@
     kr,
     zs,
     zr,
+    ps,
+    pr,
     xs,
     xrs,
     ys,
@@ -123,11 +127,8 @@
         "om1": pltpu.make_async_copy(om_hbm.at[:, 1, :], om_v.at[1], ld.at[9]),
         "slot": pltpu.make_async_copy(slot_hbm, slot_ref, ld.at[10]),
     }
-    for name in ("w", "od", "x", "g", "m", "v", "gp0", "gp1", "om0", "om1", "slot"):
+    for name in ("w", "g"):
         loads[name].start()
-
-    loads["w"].wait()
-    wb_v[...] = w_v[...].astype(BF16)
     pl.semaphore_wait(barrier, count)
 
     sends = []
@@ -153,20 +154,30 @@
         order = (first, second, 3 - first - second)
     else:
         order = tuple(range(per_row))
-    for n, j in enumerate(order):
-        at = per_row * row + j
-        for d in (2, 3, 1):
-            copy = pltpu.make_async_remote_copy(
-                src_ref=g_hbm.at[pl.ds(pl.multiple_of(j * blk, blk), blk)],
-                dst_ref=g_v.at[pl.ds(pl.multiple_of(at * blk, blk), blk)],
-                send_sem=gs.at[n, d - 1],
-                recv_sem=gr.at[at],
-                device_id=(rep, row_peer[d], col),
-                device_id_type=MESH,
-            )
-            copy.start()
-            sends.append(copy)
-
+
+    def send_blocks(urgent):
+        for n, j in enumerate(order):
+            at = per_row * row + j
+            far = (at - col - ncol // 2 + 2 * ncol) % ncol
+            near = jnp.where(far <= 1, 1, jnp.where(far == ncol - 1, 1, 0))
+            for d in (2, 3, 1):
+                copy = pltpu.make_async_remote_copy(
+                    src_ref=g_hbm.at[pl.ds(pl.multiple_of(j * blk, blk), blk)],
+                    dst_ref=g_v.at[pl.ds(pl.multiple_of(at * blk, blk), blk)],
+                    send_sem=gs.at[n, d - 1],
+                    recv_sem=gr.at[at],
+                    device_id=(rep, row_peer[d], col),
+                    device_id_type=MESH,
+                )
+                if urgent:
+                    keep(copy)
+                pl.when(near == (1 if urgent else 0))(copy.start)
+
+    send_blocks(True)
+    for name in ("od", "x", "m", "v", "gp0", "gp1", "om0", "om1", "slot"):
+        loads[name].start()
+    loads["w"].wait()
+    wb_v[...] = w_v[...].astype(BF16)
 
     def await_block(t):
         rows = pl.ds(pl.multiple_of(t * blk, blk), blk)
@@ -198,10 +209,25 @@
             preferred_element_type=F32,
         )
 
-    long, short = ncol // 2, ncol - 1 - ncol // 2
-    chains = tuple(
-        ((i + n) % 2, i, long if n == 0 else short) for n in range(2) for i in range(PIECES)
-    )
+    hops = ncol // 2 - 1
+    chains = ((0, 1), (1, 0), (0, 0), (1, 1))
+
+    def lend_copy(n, way, src, dst):
+        return pltpu.make_async_remote_copy(
+            src_ref=src,
+            dst_ref=dst,
+            send_sem=ps.at[n, way],
+            recv_sem=pr.at[n, way],
+            device_id=(rep, row, right if way == 0 else left),
+            device_id_type=MESH,
+        )
+
+    def lend_weight(way):
+        return lend_copy(0, way, wb_v.at[way * fh : (way + 1) * fh], wn_v.at[way])
+
+    def lend_block(way):
+        t = (col + ncol // 2) % ncol
+        return lend_copy(1, way, g_v.at[pl.ds(pl.multiple_of(t * blk, blk), blk)], gx_v.at[way])
 
     chunk = 80 if piece % 80 == 0 else piece
     mine = pl.ds(pl.multiple_of(yy * piece, piece), piece)
@@ -272,6 +298,8 @@
             ng_o[here, :] = held - OUTER_RATE * (average + NESTEROV * new_outer)
 
     def kv_parts(which):
+        if 1 in which:
+            loads["x"].wait()
         for d in which:
             to = row_peer[d] if d else row
             rows = pl.ds(pl.multiple_of(to * rtok, rtok), rtok)
@@ -313,22 +341,28 @@
 
         return run
 
+    for way in range(2):
+        keep(lend_weight(way)).start()
+
     outer_scatter()
-    loads["x"].wait()
-    kv_parts((3, 1))
     loads["g"].wait()
+    need(ncol // 2)
+    for way in range(2):
+        keep(lend_block(way)).start()
+    send_blocks(False)
 
     fill = {
-        (0, 3): functools.partial(kv_parts, (2, 0)),
-        (1, 1): kv_cross,
-        (1, 3): outer_pair,
+        (0, 3): functools.partial(kv_parts, (3, 1)),
+        (1, 0): functools.partial(kv_parts, (2, 0)),
+        (1, 2): kv_cross,
+        (2, 0): outer_pair,
         (2, 1): keys_values,
-        (2, 2): optimizer(0),
-        (2, 3): outer_gather,
+        (2, 2): outer_gather,
+        (2, 3): optimizer(0),
         (3, 0): optimizer(1),
         (3, 1): optimizer(2),
         (3, 2): optimizer(3),
-        (4, 2): outer_merge,
+        (4, 3): outer_merge,
     }
 
     def chain_copy(n, way, k, src):
@@ -341,35 +375,36 @@
             device_id_type=MESH,
         )
 
-    for k in range(long):
-        for n, (way, h, length) in enumerate(chains):
-            if k >= length:
-                continue
-            sign = 1 if way == 0 else -1
-            need(sign * (length - k))
-            part = contribution((col + sign * (length - k) + ncol) % ncol, h)
+    for k in range(hops):
+        for n, (way, h) in enumerate(chains):
+            away = (1 if way == 0 else -1) * (hops - k)
+            need(away)
+            part = contribution((col + away + ncol) % ncol, h)
             if k == 0:
+                if way == h:
+                    lend_weight(way).wait_recv()
+                    lend_block(way).wait_recv()
+                    part = part + lax.dot_general(
+                        gx_v[way], wn_v[way], (((1,), (1,)), ((), ())), preferred_element_type=F32
+                    )
                 zs_buf[n] = part.astype(BF16)
                 copy = chain_copy(n, way, k, zs_buf.at[n])
             else:
                 chain_copy(n, way, k - 1, zr_buf.at[n, k - 1]).wait_recv()
                 zr_buf[n, k - 1] = (zr_buf[n, k - 1].astype(F32) + part).astype(BF16)
                 copy = chain_copy(n, way, k, zr_buf.at[n, k - 1])
-            copy.start()
-            sends.append(copy)
-            at = (k, 2 * n // PIECES)
-            if 2 * n % PIECES == 0 and at in fill:
-                fill.pop(at)()
+            keep(copy).start()
+            if (k, n) in fill:
+                fill.pop((k, n))()
     for run in fill.values():
         run()
 
     need(0)
-    for h in range(PIECES):
+    for h, pair in ((1, (0, 3)), (0, (1, 2))):
         part = contribution(col, h)
-        for n in (h + PIECES, h):
-            way, _, length = chains[n]
-            chain_copy(n, way, length - 1, zr_buf.at[n, length - 1]).wait_recv()
-            part = part + zr_buf[n, length - 1].astype(F32)
+        for n in pair:
+            chain_copy(n, chains[n][0], hops - 1, zr_buf.at[n, hops - 1]).wait_recv()
+            part = part + zr_buf[n, hops - 1].astype(F32)
         ig_o[:, h * fh : (h + 1) * fh] = part.astype(BF16)
     for copy in sends:
         copy.wait_send()
@@ -392,7 +427,7 @@
     orow = outer_delta.shape[1] // LANES
     ny = nrep // 2
     piece = orow // ny
-    long = ncol // 2
+    hops = ncol // 2 - 1
     held = global_params.reshape(2, orow, LANES).transpose(1, 0, 2)
     moment = outer_moment.reshape(2, orow, LANES).transpose(1, 0, 2)
     any_ref = pl.BlockSpec(memory_space=pl.ANY)
@@ -427,7 +462,9 @@
             vmem((3, rtok, hd), BF16),
             vmem((rtok, hd), BF16),
             vmem((2 * PIECES, blk, feat // PIECES), BF16),
-            vmem((2 * PIECES, long, blk, feat // PIECES), BF16),
+            vmem((2 * PIECES, hops, blk, feat // PIECES), BF16),
+            vmem((2, feat // PIECES, hd), BF16),
+            vmem((2, blk, hd), BF16),
             vmem((orow, LANES), BF16),
             vmem((piece, LANES), BF16),
             vmem((piece, LANES), BF16),
@@ -439,8 +476,10 @@
             dma((ncol,)),
             dma((3,)),
             dma((3,)),
-            dma((2 * PIECES, long)),
-            dma((2 * PIECES, long)),
+            dma((2 * PIECES, hops)),
+            dma((2 * PIECES, hops)),
+            dma((2, 2)),
+            dma((2, 2)),
             dma((1,)),
             dma((1,)),
             dma((2, max(ny - 1, 1))),

time: 58.9 us -> 56.4 us (0.958)
  Pallas kernels: 56.8 us -> 54.6 us
    pallas_call x1, Pallas kernels: 55 us -> 52.9 us  [on_device(): pl.pallas_call(functools.partial(step_kernel, sizes), out_shape=[vmem(o.s...]
where the time goes in v3:
time: 56.4 us; the launch traced here: 55.9 us
  Pallas kernels  54.6 us (97%)
  between operations  1.29 us (2%)
    pallas_call x1, Pallas kernels, on_device(): pl.pallas_call(functools.partial(step_kernel, sizes), out_shape=[vmem(o.s...  52.9 us
    pallas_call x1, Pallas kernels, on_device(): pl.pallas_call(write_kernel, out_shape=results, in_specs=[pl.BlockSpec(me...  1.75 us

profile of v3, /device:TPU:6, one launch (start us, length us, event | category | flops | bytes accessed | tf_op | source)
XLA Modules:
  0.0 55.9 jit_solution(1983298879380256105)
XLA Ops:
  1.3 52.9 %diloco_step.1 = (bf16[384,128]{1,0:T(8,128)(2,1)S(1)}, bf16[128,1024]{1,0:T(8,128)(2,1)S(1)}, f32[1024,128]{1,0:T(8,128)S(1)}, f32[1024,128]{1,0:T(8,128)S(1)},...) custom-call(bf16[1536,1024]{1,0:T(8,128)(2,1)} %x_hbm.1, bf16[384,128]{1,0:T(8,128)(2,1)} %g_hbm.1, ...), custom_call_target="tpu_custom_call" | custom-call | tf_op jit(solution)/shard_map/diloco_step/pallas_call | solution.py:446
  54.1 1.8 %write_out.1 = (bf16[384,128]{1,0:T(8,128)(2,1)}, bf16[128,1024]{1,0:T(8,128)(2,1)}, f32[1024,128]{1,0:T(8,128)}, f32[1024,128]{1,0:T(8,128)}, f32[1024,128]{1,0...) custom-call(bf16[384,128]{1,0:T(8,128)(2,1)S(1)} %get-tuple-element.21.refs_0_, ...), custom_call_target="tpu_custom_call" | custom-call | tf_op jit(solution)/shard_map/write_out/pallas_call | solution.py:501

commit v4 on v3

--- a/solution.py
+++ b/solution.py
@@ -129,6 +129,8 @@
     }
     for name in ("w", "g"):
         loads[name].start()
+    loads["w"].wait()
+    wb_v[...] = w_v[...].astype(BF16)
     pl.semaphore_wait(barrier, count)
 
     sends = []
@@ -173,11 +175,24 @@
                     keep(copy)
                 pl.when(near == (1 if urgent else 0))(copy.start)
 
+    def lend_copy(n, way, src, dst):
+        return pltpu.make_async_remote_copy(
+            src_ref=src,
+            dst_ref=dst,
+            send_sem=ps.at[n, way],
+            recv_sem=pr.at[n, way],
+            device_id=(rep, row, right if way == 0 else left),
+            device_id_type=MESH,
+        )
+
+    def lend_weight(way):
+        return lend_copy(0, way, wb_v.at[way * fh : (way + 1) * fh], wn_v.at[way])
+
+    for way in range(2):
+        keep(lend_weight(way)).start()
     send_blocks(True)
     for name in ("od", "x", "m", "v", "gp0", "gp1", "om0", "om1", "slot"):
         loads[name].start()
-    loads["w"].wait()
-    wb_v[...] = w_v[...].astype(BF16)
 
     def await_block(t):
         rows = pl.ds(pl.multiple_of(t * blk, blk), blk)
@@ -211,19 +226,6 @@
 
     hops = ncol // 2 - 1
     chains = ((0, 1), (1, 0), (0, 0), (1, 1))
-
-    def lend_copy(n, way, src, dst):
-        return pltpu.make_async_remote_copy(
-            src_ref=src,
-            dst_ref=dst,
-            send_sem=ps.at[n, way],
-            recv_sem=pr.at[n, way],
-            device_id=(rep, row, right if way == 0 else left),
-            device_id_type=MESH,
-        )
-
-    def lend_weight(way):
-        return lend_copy(0, way, wb_v.at[way * fh : (way + 1) * fh], wn_v.at[way])
 
     def lend_block(way):
         t = (col + ncol // 2) % ncol
@@ -341,9 +343,6 @@
 
         return run
 
-    for way in range(2):
-        keep(lend_weight(way)).start()
-
     outer_scatter()
     loads["g"].wait()
     need(ncol // 2)
@@ -355,10 +354,10 @@
         (0, 3): functools.partial(kv_parts, (3, 1)),
         (1, 0): functools.partial(kv_parts, (2, 0)),
         (1, 2): kv_cross,
-        (2, 0): outer_pair,
-        (2, 1): keys_values,
-        (2, 2): outer_gather,
-        (2, 3): optimizer(0),
+        (2, 0): keys_values,
+        (2, 1): outer_pair,
+        (2, 2): optimizer(0),
+        (2, 3): outer_gather,
         (3, 0): optimizer(1),
         (3, 1): optimizer(2),
         (3, 2): optimizer(3),
@@ -411,7 +410,12 @@
 
 
 def write_kernel(*refs):
-    copies = [pltpu.make_async_copy(refs[n], refs[7 + n], refs[14].at[n]) for n in range(7)]
+    copies = []
+    for n in (6, 5, 4, 3, 2, 1, 0):
+        rows = refs[n].shape[0] // 4
+        for i in range(4):
+            part = pl.ds(i * rows, rows)
+            copies.append(pltpu.make_async_copy(refs[n].at[part], refs[7 + n].at[part], refs[14].at[n, i]))
     for copy in copies:
         copy.start()
     for copy in copies:
@@ -503,7 +507,7 @@
         out_shape=results,
         in_specs=[pl.BlockSpec(memory_space=vmem)] * 7,
         out_specs=[any_ref] * 7,
-        scratch_shapes=[dma((7,))],
+        scratch_shapes=[dma((7, 4))],
         name="write_out",
     )(*(pltpu.with_memory_space_constraint(o, vmem) for o in outs))
     keys_values, input_grad, new_weight, new_first, new_second, new_global, new_outer = outs

time: 56.4 us -> 56.2 us (level)
  no operation moved by 1% of the time
where the time goes in v4:
time: 56.2 us; the launch traced here: 56.1 us
  Pallas kernels  54.8 us (98%)
  between operations  1.29 us (2%)
    pallas_call x1, Pallas kernels, on_device(): pl.pallas_call(functools.partial(step_kernel, sizes), out_shape=[vmem(o.s...  52.9 us
    pallas_call x1, Pallas kernels, on_device(): pl.pallas_call(write_kernel, out_shape=results, in_specs=[pl.BlockSpec(me...  1.91 us

profile of v4, /device:TPU:6, one launch (start us, length us, event | category | flops | bytes accessed | tf_op | source)
XLA Modules:
  0.0 56.1 jit_solution(6137872149550876182)
XLA Ops:
  1.3 52.9 %diloco_step.1 = (bf16[384,128]{1,0:T(8,128)(2,1)S(1)}, bf16[128,1024]{1,0:T(8,128)(2,1)S(1)}, f32[1024,128]{1,0:T(8,128)S(1)}, f32[1024,128]{1,0:T(8,128)S(1)},...) custom-call(bf16[1536,1024]{1,0:T(8,128)(2,1)} %x_hbm.1, bf16[384,128]{1,0:T(8,128)(2,1)} %g_hbm.1, ...), custom_call_target="tpu_custom_call" | custom-call | tf_op jit(solution)/shard_map/diloco_step/pallas_call | solution.py:450
  54.1 1.9 %write_out.1 = (bf16[384,128]{1,0:T(8,128)(2,1)}, bf16[128,1024]{1,0:T(8,128)(2,1)}, f32[1024,128]{1,0:T(8,128)}, f32[1024,128]{1,0:T(8,128)}, f32[1024,128]{1,0...) custom-call(bf16[384,128]{1,0:T(8,128)(2,1)S(1)} %get-tuple-element.21.refs_0_, ...), custom_call_target="tpu_custom_call" | custom-call | tf_op jit(solution)/shard_map/write_out/pallas_call | solution.py:505
